TPU v7x, 32 devices: a whole 2x2x4 slice. The times are simulated.
32 devices in a mesh: head: 4 (over y, x), tok: 8 (over z, core).
Axes of the slice: x: 2, y: 2, z: 4, core: 2. Of those that a mesh axis runs over, the one named last changes fastest.
Arguments:
- queries: bfloat16 [2, 2048, 5120], P(None, 'tok', 'head'), may hold values from -6 to 6
- key_rows: bfloat16 [2048, 5120], P('tok', 'head'), may hold values from -6 to 6
- value_rows: bfloat16 [2048, 5120], P('tok', 'head'), may hold values from -6 to 6
- step_rates: float32 [20, 2048], P('head', 'tok'), may hold values from 0.05 to 1
- gate_fast: float32 [20, 256, 256], P('head'), may hold values from -0.375 to 0.375
- up_fast: float32 [20, 256, 256], P('head'), may hold values from -0.375 to 0.375
- down_fast: float32 [20, 256, 256], P('head'), may hold values from -0.375 to 0.375
Outputs:
- out_rows: bfloat16 [2, 2048, 5120], P(None, ('tok', 'head'))
All inputs are finite; a program needn't handle non-finite values.
Results may differ from a plain program's by a relative error of at most 0.011.
Values may be sent and summed in bfloat16 or wider, within the bound.
A program may use at most 64 MiB of HBM per device.

v0:
```python
import jax
import jax.numpy as jnp
from jax import lax
from jax.sharding import PartitionSpec as P

NS_STEPS = 3


coef_first = 3.4445
coef_second = -4.775
coef_third = 2.0315


def fast_apply(inputs, gate_mat, up_mat, down_mat):
    gate_pre = jnp.einsum("thd,hdf->thf", inputs, gate_mat, preferred_element_type=jnp.float32)
    up_pre = jnp.einsum("thd,hdf->thf", inputs, up_mat, preferred_element_type=jnp.float32)
    hidden = (jax.nn.silu(gate_pre) * up_pre).astype(jnp.bfloat16)
    result = jnp.einsum("thf,hfd->thd", hidden, down_mat, preferred_element_type=jnp.float32)
    return result.astype(jnp.bfloat16).reshape(inputs.shape[0], -1)


def orthogonal(gradient):
    scale = jnp.sqrt(jnp.sum(gradient * gradient, axis=(1, 2), keepdims=True)) + 1e-07
    iterate = gradient / scale
    for sweep in range(NS_STEPS):
        gram = jnp.einsum("hdf,hdg->hfg", iterate, iterate, precision=lax.Precision.HIGHEST)
        square = jnp.einsum("hfg,hgk->hfk", gram, gram, precision=lax.Precision.HIGHEST)
        poly = coef_second * gram + coef_third * square
        iterate = coef_first * iterate + jnp.einsum(
            "hdf,hfg->hdg", iterate, poly, precision=lax.Precision.HIGHEST
        )
    return iterate


def local(queries, key_rows, value_rows, step_rates, gate_fast, up_fast, down_fast):
    heads_here = gate_fast.shape[0]
    head_size = gate_fast.shape[1]
    local_rows = key_rows.shape[0]
    gate_half = gate_fast.astype(jnp.bfloat16)
    up_half = up_fast.astype(jnp.bfloat16)
    down_half = down_fast.astype(jnp.bfloat16)
    query_heads = queries.reshape(2, local_rows, heads_here, head_size)
    first_out = fast_apply(query_heads[0], gate_half, up_half, down_half)
    key_heads = key_rows.reshape(local_rows, heads_here, head_size)
    value_heads = value_rows.reshape(local_rows, heads_here, head_size)
    gate_pre = jnp.einsum("thd,hdf->thf", key_heads, gate_half, preferred_element_type=jnp.float32)
    up_pre = jnp.einsum("thd,hdf->thf", key_heads, up_half, preferred_element_type=jnp.float32)
    sigmoid_gate = jax.nn.sigmoid(gate_pre)
    silu_gate = jax.nn.silu(gate_pre)
    hidden = (silu_gate * up_pre).astype(jnp.bfloat16)
    rates = jnp.transpose(step_rates)[:, :, None]
    down_in = (-(rates * value_heads.astype(jnp.float32))).astype(jnp.bfloat16)
    down_grad = jnp.einsum("thf,thd->hfd", hidden, down_in, preferred_element_type=jnp.float32)
    hidden_grad = jnp.einsum("thd,hfd->thf", down_in, down_half, preferred_element_type=jnp.float32)
    up_in = (hidden_grad * silu_gate).astype(jnp.bfloat16)
    gate_in = (
        hidden_grad * up_pre * sigmoid_gate * (1.0 + gate_pre * (1.0 - sigmoid_gate))
    ).astype(jnp.bfloat16)
    gate_grad = jnp.einsum("thd,thf->hdf", key_heads, gate_in, preferred_element_type=jnp.float32)
    up_grad = jnp.einsum("thd,thf->hdf", key_heads, up_in, preferred_element_type=jnp.float32)
    stacked = jnp.concatenate((gate_grad, up_grad, down_grad), 0)
    matrix_count = stacked.shape[0]
    tok_width = lax.axis_size("tok")
    per_device = -(-matrix_count // tok_width)
    pad_rows = per_device * tok_width - matrix_count
    stacked = jnp.pad(stacked, ((0, pad_rows), (0, 0), (0, 0)))
    summed_share = lax.psum_scatter(stacked, "tok", scatter_dimension=0, tiled=True)
    fast_all = jnp.pad(
        jnp.concatenate((gate_fast, up_fast, down_fast), 0), ((0, pad_rows), (0, 0), (0, 0))
    )
    fast_share = lax.dynamic_slice_in_dim(
        fast_all, lax.axis_index("tok") * per_device, per_device, 0
    )
    next_share = (fast_share - orthogonal(summed_share)).astype(jnp.bfloat16)
    next_all = lax.all_gather(next_share, "tok", axis=0, tiled=True)
    gate_next = next_all[:heads_here]
    up_next = next_all[heads_here : 2 * heads_here]
    down_next = next_all[2 * heads_here : 3 * heads_here]
    second_out = fast_apply(query_heads[1], gate_next, up_next, down_next)
    return lax.all_to_all(
        jnp.stack((first_out, second_out), 0), "head", split_axis=1, concat_axis=2, tiled=True
    )


def solution(mesh):
    placed = (
        P(None, "tok", "head"),
        P("tok", "head"),
        P("tok", "head"),
        P("head", "tok"),
        P("head", None, None),
        P("head", None, None),
        P("head", None, None),
    )
    return jax.shard_map(
        local, mesh=mesh, in_specs=placed, out_specs=P(None, ("tok", "head"), None), check_vma=False
    )
```

profile of v0, /device:TPU:0, one launch (start us, length us, event | category | flops | bytes accessed | tf_op | source)
XLA Modules:
  0.0 148.3 jit_solution(8281958838822265854)
XLA Ops:
  6.5 0.0 copy-start
  6.5 0.0 reduce-scatter.2.cloned.1.call-start
  6.5 1.4 copy.119
  8.0 0.1 copy-done
  8.0 0.0 copy-start.1
  8.1 1.4 convolution_bitcast_fusion.3
  9.5 0.0 copy-done.1
  9.5 1.4 convolution_bitcast_fusion.4
  10.9 0.0 copy-start.11
  10.9 2.2 %copy.116 = bf16[256,1280]{0,1:T(8,128)(2,1)} copy(bf16[256,1280]{1,0:T(8,128)(2,1)} %param.9) | data formatting | bytes 1310720 | tf_op args[2]
  13.1 0.0 copy-done.11
  13.1 0.0 copy-start.7
  13.1 1.9 %convolution_bitcast_fusion = f32[256,5,256]{0,2,1:T(8,128)S(1)} fusion(bf16[256,5,256]{0,2,1:T(8,128)(2,1)} %bitcast.77, f32[256,5]{0,1:T(8,128)S(1)} %bitcast.85, f32[5,256,256]{2,1,0:T(8,128)} %param.13), kind=kOutput, calls=%fused_computation.6 | convolution fusion | flops 169410560 | bytes 3281920 | tf_op jit(solution)/shard_map/thd,hfd->thf/dot_general | solution.py:54
  15.1 0.0 copy-done.7
  15.1 0.0 copy-start.8
  15.1 0.5 convolution_bitcast_fusion.1
  15.6 0.8 copy-done.8
  16.4 0.7 convolution_bitcast_fusion.2
  17.1 0.4 copy-done.5
  17.5 0.6 fusion.12
  18.1 2.5 %select_maximum_fusion = f32[16,256,256]{1,2,0:T(8,128)} fusion(f32[5,256,256]{1,2,0:T(8,128)S(1)} %fusion.12, f32[5,256,256]{1,2,0:T(8,128)S(1)} %convolution_bitcast_fusion.1, f32[5,256,256]{1,2,0:T(8,128)S(1)} %convolution_bitcast_fusion.2), kind=kLoop, calls=%fused_computation | loop fusion | flops 6291456 | bytes 8126464 | tf_op jit(solution)/shard_map/concatenate | solution.py:61
  20.6 0.0 reduce-scatter.2.cloned.1.call-update
  20.6 0.2 all-gather.2.cloned.1.call-start
  20.9 1.5 copy.113
  22.3 1.5 %copy.114 = f32[5,256,256]{1,2,0:T(8,128)} copy(f32[5,256,256]{2,1,0:T(8,128)S(1)} %copy-done.1) | data formatting | bytes 2621440 | tf_op args[5]
  23.8 2.8 %copy.115 = f32[5,256,256]{1,2,0:T(8,128)} copy(f32[5,256,256]{2,1,0:T(8,128)} %param.13) | data formatting | bytes 2621440 | tf_op args[6]
  26.6 46.8 %reduce-scatter.2.cloned.1.call-done = f32[2,256,256]{1,2,0:T(8,128)} async-done(((f32[16,256,256]{1,2,0:T(8,128)}), f32[2,256,256]{1,2,0:T(8,128)}) %reduce-scatter.2.cloned.1.call-update) | async-done | bytes 524304 | tf_op jit(solution)/shard_map/reduce_scatter | solution.py:67
  73.4 1.2 multiply_reduce_fusion
  74.6 2.0 %fusion.30 = f32[2,256,256]{2,1,0:T(8,128)S(1)} fusion(f32[2,256,256]{1,2,0:T(8,128)} %reduce-scatter.2.cloned.1.call-done, f32[2]{0:T(128)S(1)} %sqrt_add_fusion), kind=kOutput, calls=%fused_computation.57 | convolution fusion | flops 402784256 | bytes 1048584 | tf_op jit(solution)/shard_map/hdf,hdg->hfg/dot_general | solution.py:26
  76.7 0.7 fusion.10
  77.4 0.0 copy-done.10
  77.4 1.1 convolution_add_fusion.2
  78.5 0.7 fusion.36
  79.1 0.7 fusion.9
  79.8 0.0 copy-start.4
  79.8 1.0 convolution_add_fusion.1
  80.9 0.0 copy-start.2
  80.9 0.0 copy-start.3
  80.9 0.7 fusion.37
  81.6 0.7 fusion.8
  82.3 0.0 copy-done.4
  82.3 0.0 copy-done.2
  82.3 0.4 copy-done.3
  82.7 1.2 fusion.11
  83.8 0.8 copy.137
  84.7 0.0 all-gather.2.cloned.1.call-update
  84.7 2.2 %fusion.35 = (bf16[1,256,1280]{2,1,0:T(8,128)(2,1)S(1)}, bf16[1,256,1280]{2,1,0:T(8,128)(2,1)}) fusion(bf16[2,256,1280]{2,1,0:T(8,128)(2,1)} %param.7), kind=kLoop, calls=%fused_computation.63 | loop fusion | bytes 2621440 | tf_op jit(solution)/shard_map/slice | solution.py:43
  86.9 2.2 %copy.180 = bf16[1,256,1280]{1,2,0:T(8,128)(2,1)} copy(bf16[1,256,1280]{2,1,0:T(8,128)(2,1)} %get-tuple-element.6) | data formatting | bytes 1310720
  89.1 1.1 copy.177
  90.1 2.6 %convolution_bitcast_fusion.6 = f32[256,5,256]{0,2,1:T(8,128)} fusion(bf16[256,5,256]{0,2,1:T(8,128)(2,1)} %bitcast.79, f32[5,256,256]{2,1,0:T(8,128)S(1)} %copy-done), kind=kOutput, calls=%fused_computation.12 | convolution fusion | flops 168099840 | bytes 3276800 | tf_op jit(solution)/shard_map/thd,hdf->thf/dot_general | solution.py:15
  92.7 0.0 copy-done.6
  92.7 3.3 %convolution_convert_fusion.1 = bf16[5,256,256]{1,2,0:T(8,128)(2,1)} fusion(bf16[256,5,256]{0,2,1:T(8,128)(2,1)S(1)} %bitcast.80, f32[256,5,256]{0,2,1:T(8,128)} %convolution_bitcast_fusion.6, f32[5,256,256]{2,1,0:T(8,128)} %param.13, f32[5,256,256]{2,1,0:T(8,128)S(1)} %copy-done.1), kind=kOutput, calls=%fused_computation.20 | convolution fusion | flops 338493440 | bytes 5242880 | tf_op jit(solution)/shard_map/thf,hfd->thd/dot_general | solution.py:18
  96.1 2.7 %copy.145 = bf16[1,256,1280]{2,0,1:T(2,128)(2,1)S(1)} copy(bf16[1,256,1280]{1,2,0:T(8,128)(2,1)} %bitcast.83) | data formatting | bytes 1310720 | tf_op jit(solution)/shard_map/stack;reshape | solution.py:81
  98.7 13.7 %all-gather.2.cloned.1.call-done = bf16[16,256,256]{2,1,0:T(8,128)(2,1)} async-done(((bf16[2,256,256]{2,1,0:T(8,128)(2,1)}), bf16[16,256,256]{2,1,0:T(8,128)(2,1)}) %all-gather.2.cloned.1.call-update) | async-done | bytes 2097168 | tf_op jit(solution)/shard_map/all_gather | solution.py:75
  112.5 0.0 copy-done.9
  112.5 1.6 %convolution_bitcast_fusion.8 = f32[256,5,256]{0,2,1:T(8,128)S(1)} fusion(bf16[16,256,256]{2,1,0:T(8,128)(2,1)} %all-gather.2.cloned.1.call-done, bf16[256,5,256]{0,2,1:T(8,128)(2,1)S(1)} %bitcast.81), kind=kOutput, calls=%fused_computation.16 | convolution fusion | flops 167772160 | bytes 4063232 | tf_op jit(solution)/shard_map/thd,hdf->thf/dot_general | solution.py:15
  114.1 0.2 copy-done.12
  114.3 0.6 fusion.2
  114.8 0.4 convolution_convert_fusion
  115.2 1.1 copy.146
  116.4 3.0 %pad_maximum_fusion = bf16[2,256,1280]{2,0,1:T(2,128)(2,1)S(1)} fusion(bf16[1,256,1280]{2,0,1:T(2,128)(2,1)S(1)} %copy.146, bf16[1,256,1280]{2,0,1:T(2,128)(2,1)S(1)} %copy.145), kind=kLoop, calls=%fused_computation.21 | loop fusion | flops 2621440 | bytes 2621440 | tf_op jit(solution)/shard_map/stack | solution.py:81
  119.3 20.8 %all_to_all.18 = bf16[2,256,1280]{2,0,1:T(2,128)(2,1)S(1)} all-to-all(bf16[2,256,1280]{2,0,1:T(2,128)(2,1)S(1)} %pad_maximum_fusion), channel_id=1, replica_groups=mesh['head'=4,'tok'=8] {'head'}, dimensions={1} | all-to-all | bytes 2621440 | tf_op jit(solution)/shard_map/all_to_all | solution.py:80
  140.1 0.1 copy.147
  140.3 1.2 copy.182
  (6 shorter events, 0.0 us)
Async XLA Ops:
  6.5 1.5 %copy-start = (f32[5,256,256]{2,1,0:T(8,128)S(1)}, f32[5,256,256]{2,1,0:T(8,128)}, u32[]{:S(2)}) copy-start(f32[5,256,256]{2,1,0:T(8,128)} %param.11) | copy-start | bytes 3932164
  6.5 66.9 %reduce-scatter.2.cloned.1.call-start = ((), (), s32[]{:S(2)}) async-start(), calls=%async_computation.2 | async-start | bytes 4718592 | tf_op jit(solution)/shard_map/reduce_scatter | solution.py:67
  8.0 1.5 copy-start.1
  10.9 2.2 %copy-start.11 = (f32[5,256]{1,0:T(8,128)S(1)}, f32[5,256]{1,0:T(8,128)}, u32[]{:S(2)}) copy-start(f32[5,256]{1,0:T(8,128)} %param.10) | copy-start | bytes 15364
  13.1 2.0 %copy-start.7 = (f32[256,5,256]{0,2,1:T(8,128)S(1)}, f32[256,5,256]{0,2,1:T(8,128)}, u32[]{:S(2)}) copy-start(f32[256,5,256]{0,2,1:T(8,128)} %convolution_bitcast_fusion.3) | copy-start | bytes 3932164
  15.1 1.3 copy-start.8
  16.4 1.1 copy-start.5
  20.6 91.9 %all-gather.2.cloned.1.call-start = ((), (), s32[]{:S(2)}) async-start(), calls=%async_computation.3 | async-start | bytes 2359296 | tf_op jit(solution)/shard_map/all_gather | solution.py:75
  74.6 2.7 %copy-start.10 = (f32[2,256,256]{1,2,0:T(8,128)S(1)}, f32[2,256,256]{1,2,0:T(8,128)}, u32[]{:S(2)}) copy-start(f32[2,256,256]{1,2,0:T(8,128)} %reduce-scatter.2.cloned.1.call-done) | copy-start | bytes 1572868
  79.8 2.5 %copy-start.4 = (f32[5,256,256]{1,2,0:T(8,128)S(1)}, f32[5,256,256]{1,2,0:T(8,128)}, u32[]{:S(2)}) copy-start(f32[5,256,256]{1,2,0:T(8,128)} %copy.115) | copy-start | bytes 3932164
  80.9 1.4 copy-start.2
  80.9 1.8 %copy-start.3 = (f32[5,256,256]{1,2,0:T(8,128)S(1)}, f32[5,256,256]{1,2,0:T(8,128)}, u32[]{:S(2)}) copy-start(f32[5,256,256]{1,2,0:T(8,128)} %copy.114) | copy-start | bytes 3932164
  90.1 2.6 %copy-start.6 = (bf16[1,256,1280]{1,2,0:T(8,128)(2,1)S(1)}, bf16[1,256,1280]{1,2,0:T(8,128)(2,1)}, u32[]{:S(2)}) copy-start(bf16[1,256,1280]{1,2,0:T(8,128)(2,1)} %copy.177) | copy-start | bytes 1966084
  96.1 16.4 %copy-start.9 = (bf16[1,256,1280]{1,2,0:T(8,128)(2,1)S(1)}, bf16[1,256,1280]{1,2,0:T(8,128)(2,1)}, u32[]{:S(2)}) copy-start(bf16[1,256,1280]{1,2,0:T(8,128)(2,1)} %copy.180) | copy-start | bytes 1966084
  112.5 1.8 %copy-start.12 = (bf16[16,256,256]{2,1,0:T(8,128)(2,1)S(1)}, bf16[16,256,256]{2,1,0:T(8,128)(2,1)}, u32[]{:S(2)}) copy-start(bf16[16,256,256]{2,1,0:T(8,128)(2,1)} %all-gather.2.cloned.1.call-done) | copy-start | bytes 6291460
Sparse Core Ops, SparseCore 0:
  20.7 52.6 reduce-scatter.1
  84.8 27.6 all-gather.1
where the time goes:
time: 149 us; the launch traced here: 148 us
  waiting for transfers between devices  60.6 us (41%)
  matrix products  23.8 us (16%)
  local copies, waits for them, and re-layouts  22.6 us (15%)
  blocking collectives  20.8 us (14%)
  between operations  13.6 us (9%)
  other arithmetic  6.65 us (4%)
    reduce_scatter x1, waiting for transfers between devices, local(): lax.psum_scatter(stacked, 'tok', scatter_dimension=0, tiled=True)  46.8 us
    all_to_all x1, blocking collectives, local(): lax.all_to_all(jnp.stack((first_out, second_out), 0), 'head', split_axis=...  20.8 us
    unnamed x33, local copies, waits for them, and re-layouts  14.4 us
    all_gather x1, waiting for transfers between devices, local(): next_all = lax.all_gather(next_share, 'tok', axis=0, tiled=True)  13.7 us
    dot_general x2, matrix products, fast_apply(): jnp.einsum('thd,hdf->thf', inputs, gate_mat, preferred_element_type=jnp.f...  4.22 us
    another operation x2, local copies, waits for them, and re-layouts, local(): jnp.stack((first_out, second_out), 0)  3.81 us
    dot_general x2, matrix products, fast_apply(): jnp.einsum('thf,hfd->thd', hidden, down_mat, preferred_element_type=jnp.f...  3.69 us
    dot_general x3, matrix products, orthogonal(): jnp.einsum('hdf,hdg->hfg', iterate, iterate, precision=lax.Precision.HIGH...  3.33 us
  transfers between devices with their start and end apart: 2, of which 2 were waited for; matrix products, arithmetic and copies ran while one was open for 13% of the time, Pallas kernels for 0%

commit v1 on v0

v1 whole, which is shorter than its diff:
```python
import functools

import jax
import jax.numpy as jnp
from jax import lax
from jax.experimental import pallas as pl
from jax.experimental.pallas import tpu as pltpu
from jax.sharding import PartitionSpec as P

NS_STEPS = 3
KINDS = 3
PIECES = 2
LAG = 2

coef_first = 3.4445
coef_second = -4.775
coef_third = 2.0315

MESH = pl.DeviceIdType.MESH
BF = jnp.bfloat16
F32 = jnp.float32


def mm(a, b):
    return jnp.dot(a, b, preferred_element_type=F32)


def mm_tn(a, b):
    return lax.dot_general(a, b, (((0,), (0,)), ((), ())), preferred_element_type=F32)


def mm_nt(a, b):
    return lax.dot_general(a, b, (((1,), (1,)), ((), ())), preferred_element_type=F32)


def fast_apply(x, gate, up, down):
    pre = mm(x, gate)
    hidden = (pre / (1.0 + jnp.exp(-pre)) * mm(x, up)).astype(BF)
    return mm(hidden, down).astype(BF)


def kernel(
    nh, nz, q_in, k_in, v_in, rates, g_in, u_in, d_in, out,
    qb, kb, vb, wf, wh, gb, pb, cs, cr, wn, ob,
    in_sem, ps_s, ps_r, ch_s, ch_r, ag_s, ag_r, ap_s, ap_r, a_s, a_r, a_l,
):
    heads, rows, size = kb.shape
    count = KINDS * heads
    pairs = pb.shape[0]
    piece = size // PIECES
    share = rows // nh
    hd = lax.axis_index("head")
    tok = lax.axis_index("tok")
    lane = lax.rem(tok, 2)
    z = tok // 2
    partner = (hd, z * 2 + 1 - lane)

    def cut(h):
        return pl.ds(h * size if isinstance(h, int) else pl.multiple_of(h * size, size), size)

    def load(at, h):
        src, dst = (
            (k_in.at[:, cut(h)], kb.at[h]),
            (g_in.at[h], wf.at[0, h]),
            (u_in.at[h], wf.at[1, h]),
            (v_in.at[:, cut(h)], vb.at[h]),
            (d_in.at[h], wf.at[2, h]),
            (q_in.at[0, :, cut(h)], qb.at[0, h]),
            (q_in.at[1, :, cut(h)], qb.at[1, h]),
        )[at]
        return pltpu.make_async_copy(src, dst, in_sem.at[at, h])

    for h in range(heads):
        for at in range(5):
            load(at, h).start()
    for h in range(heads):
        for at in (5, 6):
            load(at, h).start()

    barrier = pltpu.get_barrier_semaphore()
    pl.semaphore_signal(barrier, inc=1, device_id=partner, device_id_type=MESH)
    for p in range(1, nh):
        pl.semaphore_signal(
            barrier, inc=1, device_id=(lax.rem(hd + p, nh), tok), device_id_type=MESH
        )

    @pl.when(z > 0)
    def _():
        pl.semaphore_signal(barrier, inc=1, device_id=(hd, tok - 2), device_id_type=MESH)

    @pl.when(z < nz - 1)
    def _():
        pl.semaphore_signal(barrier, inc=1, device_id=(hd, tok + 2), device_id_type=MESH)

    inner = (z > 0).astype(jnp.int32) + (z < nz - 1).astype(jnp.int32)
    pl.semaphore_wait(barrier, nh + inner)

    def mine(j):
        return 2 * j + lane

    def side(j):
        return lax.rem(j, 2)

    def is_start(j):
        return z == (1 - side(j)) * (nz - 1)

    def is_owner(j):
        return z == side(j) * (nz - 1)

    def towards(j):
        return (hd, tok + (2 * side(j) - 1) * 2)

    def back(j):
        return (hd, tok - (2 * side(j) - 1) * 2)

    def swap(j):
        return pltpu.make_async_remote_copy(
            gb.at[2 * j + 1 - lane], pb.at[j], ps_s.at[j], ps_r.at[j],
            device_id=partner, device_id_type=MESH,
        )

    def chain(j, g):
        part = pl.ds(g * piece, piece)
        return pltpu.make_async_remote_copy(
            cs.at[j, part], cr.at[j, part], ch_s.at[j, g], ch_r.at[j, g],
            device_id=towards(j), device_id_type=MESH,
        )

    def spread(j, g):
        part = pl.ds(g * piece, piece)
        return pltpu.make_async_remote_copy(
            wn.at[mine(j), part], wn.at[mine(j), part], ag_s.at[j, g], ag_r.at[j, g],
            device_id=back(j), device_id_type=MESH,
        )

    def across(j, g, m):
        part = pl.ds(g * piece, piece)
        return pltpu.make_async_remote_copy(
            wn.at[m, part], wn.at[m, part], ap_s.at[j, g], ap_r.at[j, g],
            device_id=partner, device_id_type=MESH,
        )

    def wide(h):
        return pl.ds(pl.multiple_of((hd * heads + h) * size, size), size)

    def deal(b, h, p):
        peer = lax.rem(hd + p, nh)
        return pltpu.make_async_remote_copy(
            ob.at[b, h, pl.ds(pl.multiple_of(peer * share, share), share)],
            out.at[b, :, wide(h)],
            a_s.at[b, h, p - 1], a_r.at[b, h, p - 1],
            device_id=(peer, tok), device_id_type=MESH,
        )

    def arrive(b, h, p):
        source = lax.rem(hd + nh - p, nh)
        return pltpu.make_async_remote_copy(
            ob.at[b, h, pl.ds(pl.multiple_of(hd * share, share), share)],
            out.at[b, :, pl.ds(pl.multiple_of((source * heads + h) * size, size), size)],
            a_s.at[b, h, p - 1], a_r.at[b, h, p - 1],
            device_id=(source, tok), device_id_type=MESH,
        )

    def keep(b, h):
        return pltpu.make_async_copy(
            ob.at[b, h, pl.ds(pl.multiple_of(hd * share, share), share)],
            out.at[b, :, wide(h)], a_l.at[b, h],
        )

    def deal_all(b, h):
        for p in range(nh - 1, 0, -1):
            deal(b, h, p).start()
        keep(b, h).start()

    def wait_load(h, picks):
        for at in picks:
            load(at, h).wait()

    def gradients(h):
        wait_load(h, range(5))
        keys = kb[h]
        gate = wf[0, h].astype(BF)
        up = wf[1, h].astype(BF)
        down = wf[2, h].astype(BF)
        wh[0, h] = gate
        wh[1, h] = up
        wh[2, h] = down
        zg = mm(keys, gate)
        zu = mm(keys, up)
        sig = 1.0 / (1.0 + jnp.exp(-zg))
        silu = zg * sig
        hidden = (silu * zu).astype(BF)
        line = jnp.broadcast_to(rates[pl.ds(h, 1), :], (128, rows))
        column = jnp.transpose(line)
        column = jnp.concatenate([column] * (size // 128), axis=1)
        dout = (-(column * vb[h].astype(F32))).astype(BF)
        dh = mm_nt(dout, down)
        dzu = (dh * silu).astype(BF)
        dzg = (dh * zu * sig * (1.0 + zg * (1.0 - sig))).astype(BF)
        base = KINDS * h
        gb[base] = mm_tn(keys, dzg).astype(BF)
        gb[base + 1] = mm_tn(keys, dzu).astype(BF)
        gb[base + 2] = mm_tn(hidden, dout).astype(BF)
        for kind in range(KINDS):
            m = base + kind

            @pl.when(lax.rem(m, 2) != lane)
            def _():
                swap(m // 2).start()

    def first(h):
        wait_load(h, (5,))
        ob[0, h] = fast_apply(qb[0, h], wh[0, h], wh[1, h], wh[2, h])
        deal_all(0, h)

    def own(h, step):
        for kind in range(KINDS):
            m = KINDS * h + kind

            @pl.when(lax.rem(m, 2) == lane)
            def _():
                step(m // 2)

    def start_step(j):
        swap(j).wait_recv()

        @pl.when(is_start(j))
        def _():
            cs[j] = (gb[mine(j)].astype(F32) + pb[j].astype(F32)).astype(BF)
            for g in range(PIECES):
                chain(j, g).start()

    def pass_step(j):
        @pl.when(jnp.logical_not(is_start(j)) & jnp.logical_not(is_owner(j)))
        def _():
            for g in range(PIECES):
                part = pl.ds(g * piece, piece)
                chain(j, g).wait_recv()
                cs[j, part] = (
                    gb[mine(j), part].astype(F32)
                    + pb[j, part].astype(F32)
                    + cr[j, part].astype(F32)
                ).astype(BF)
                chain(j, g).start()

    @pl.loop(0, 2 * heads)
    def _(t):
        @pl.when(t < heads)
        def _():
            gradients(t)

        @pl.when(t >= heads)
        def _():
            first(t - heads)

        @pl.when((t >= 1) & (t <= heads))
        def _():
            own(t - 1, start_step)

        @pl.when((t >= LAG) & (t < heads + LAG))
        def _():
            own(t - LAG, pass_step)

    @pl.loop(0, pairs)
    def _(j):
        m = mine(j)

        @pl.when((m < count) & is_owner(j))
        def _():
            for g in range(PIECES):
                chain(j, g).wait_recv()
            grad = gb[m].astype(F32) + pb[j].astype(F32) + cr[j].astype(F32)
            scale = jnp.sqrt(jnp.sum(grad * grad)) + 1e-07
            x = grad / scale
            for _ in range(NS_STEPS):
                xb = x.astype(BF)
                gram = mm_tn(xb, xb)
                half = gram.astype(BF)
                poly = coef_second * gram + coef_third * mm(half, half)
                x = coef_first * x + mm(xb, poly.astype(BF))
            wn[m] = (wf[lax.rem(m, KINDS), m // KINDS] - x).astype(BF)
            for g in range(PIECES):
                spread(j, g).start()
                across(j, g, m).start()

    def second(h):
        for kind in range(KINDS):
            m = KINDS * h + kind

            @pl.when(lax.rem(m, 2) != lane)
            def _():
                for g in range(PIECES):
                    across(m // 2, g, m).wait_recv()

        @pl.when(h >= 0)
        def _():
            wait_load(h, (6,))
            base = KINDS * h
            ob[1, h] = fast_apply(qb[1, h], wn[base], wn[base + 1], wn[base + 2])
            deal_all(1, h)

    @pl.loop(0, pairs)
    def _(j):
        m = mine(j)

        @pl.when((m < count) & jnp.logical_not(is_owner(j)))
        def _():
            for g in range(PIECES):
                spread(j, g).wait_recv()

                @pl.when(jnp.logical_not(is_start(j)))
                def _():
                    spread(j, g).start()

                across(j, g, m).start()

        h = jnp.maximum(2 * j - 1, 0) // KINDS

        @pl.when((j >= 1) & (h < heads) & ((KINDS * h + KINDS - 1) // 2 == j))
        def _():
            second(h)

    @pl.loop(0, pairs)
    def _(j):
        m = mine(j)

        @pl.when(2 * j + 1 - lane < count)
        def _():
            swap(j).wait_send()

        @pl.when(m < count)
        def _():
            for g in range(PIECES):
                across(j, g, m).wait_send()

                @pl.when(jnp.logical_not(is_owner(j)))
                def _():
                    chain(j, g).wait_send()

                @pl.when(jnp.logical_not(is_start(j)))
                def _():
                    spread(j, g).wait_send()

    for b in range(2):
        @pl.loop(0, heads)
        def _(h):
            for p in range(1, nh):
                arrive(b, h, p).wait_recv()
                deal(b, h, p).wait_send()
            keep(b, h).wait()


def solution(mesh):
    nh = mesh.shape["head"]
    nz = mesh.shape["tok"] // 2

    def local(queries, key_rows, value_rows, step_rates, gate_fast, up_fast, down_fast):
        heads, size, _ = gate_fast.shape
        rows = key_rows.shape[0]
        pairs = (KINDS * heads + 1) // 2
        anywhere = pl.BlockSpec(memory_space=pl.ANY)
        dma = pltpu.SemaphoreType.DMA
        return pl.pallas_call(
            functools.partial(kernel, nh, nz),
            out_shape=jax.ShapeDtypeStruct((2, rows // nh, nh * heads * size), BF),
            in_specs=[
                anywhere, anywhere, anywhere,
                pl.BlockSpec(memory_space=pltpu.VMEM),
                anywhere, anywhere, anywhere,
            ],
            out_specs=anywhere,
            scratch_shapes=[
                pltpu.VMEM((2, heads, rows, size), BF),
                pltpu.VMEM((heads, rows, size), BF),
                pltpu.VMEM((heads, rows, size), BF),
                pltpu.VMEM((KINDS, heads, size, size), F32),
                pltpu.VMEM((KINDS, heads, size, size), BF),
                pltpu.VMEM((2 * pairs, size, size), BF),
                pltpu.VMEM((pairs, size, size), BF),
                pltpu.VMEM((pairs, size, size), BF),
                pltpu.VMEM((pairs, size, size), BF),
                pltpu.VMEM((2 * pairs, size, size), BF),
                pltpu.VMEM((2, heads, rows, size), BF),
                dma((7, heads)),
                dma((pairs,)), dma((pairs,)),
                dma((pairs, PIECES)), dma((pairs, PIECES)),
                dma((pairs, PIECES)), dma((pairs, PIECES)),
                dma((pairs, PIECES)), dma((pairs, PIECES)),
                dma((2, heads, nh - 1)), dma((2, heads, nh - 1)),
                dma((2, heads)),
            ],
            compiler_params=pltpu.CompilerParams(
                collective_id=0, has_side_effects=True, vmem_limit_bytes=48 << 20
            ),
        )(queries, key_rows, value_rows, step_rates, gate_fast, up_fast, down_fast)

    placed = (
        P(None, "tok", "head"),
        P("tok", "head"),
        P("tok", "head"),
        P("head", "tok"),
        P("head", None, None),
        P("head", None, None),
        P("head", None, None),
    )
    return jax.shard_map(
        local, mesh=mesh, in_specs=placed, out_specs=P(None, ("tok", "head"), None), check_vma=False
    )
```

time: 149 us -> 99.9 us (0.67)
  Pallas kernels: 0 us -> 93 us
  waiting for transfers between devices: 60.6 us -> 0 us
  matrix products: 23.8 us -> 0 us
  blocking collectives: 20.8 us -> 0 us
  local copies, waits for them, and re-layouts: 22.6 us -> 6.56 us
  between operations: 13.6 us -> 0.01 us
  other arithmetic: 6.65 us -> 0 us
    pallas_call x0 -> x1, Pallas kernels: none -> 93 us  [local(): pl.pallas_call(functools.partial(kernel, nh, nz), out_shape=jax.ShapeDtyp...]
    reduce_scatter x1 -> x0, waiting for transfers between devices: 46.8 us -> none  [local(): lax.psum_scatter(stacked, 'tok', scatter_dimension=0, tiled=True)]
    dot_general x20 -> x0, matrix products: 23.8 us -> none  [the longest x2 4.22 us: fast_apply(): jnp.einsum('thd,hdf->thf', inputs, gate_mat, preferred_element_type=jnp.f...]
    all_to_all x1 -> x0, blocking collectives: 20.8 us -> none  [local(): lax.all_to_all(jnp.stack((first_out, second_out), 0), 'head', split_axis=...]
    all_gather x1 -> x0, waiting for transfers between devices: 13.7 us -> none  [local(): next_all = lax.all_gather(next_share, 'tok', axis=0, tiled=True)]
    unnamed x33 -> x11, local copies, waits for them, and re-layouts: 14.4 us -> 6.56 us
    another operation x2 -> x0, local copies, waits for them, and re-layouts: 3.81 us -> none  [local(): jnp.stack((first_out, second_out), 0)]
    another operation x1 -> x0, other arithmetic: 2.97 us -> none  [local(): jnp.stack((first_out, second_out), 0)]
  transfers between devices with their start and end apart: 2 -> 0, of which waited for: 2 -> 0; matrix products, arithmetic and copies ran while one was open for 13% -> 0% of each run, Pallas kernels for 0% -> 0%
where the time goes in v1:
time: 99.9 us; the launch traced here: 99.5 us
  Pallas kernels  93 us (93%)
  local copies, waits for them, and re-layouts  6.56 us (7%)
    pallas_call x1, Pallas kernels, local(): pl.pallas_call(functools.partial(kernel, nh, nz), out_shape=jax.ShapeDtyp...  93 us
    unnamed x11, local copies, waits for them, and re-layouts  6.56 us

profile of v1, /device:TPU:0, one launch (start us, length us, event | category | flops | bytes accessed | tf_op | source)
XLA Modules:
  0.0 99.5 jit_solution(5194821601775430408)
XLA Ops:
  0.0 0.0 copy-start
  0.0 1.3 %copy-done = bf16[2,256,1280]{2,1,0:T(8,128)(2,1)S(1)} copy-done((bf16[2,256,1280]{2,1,0:T(8,128)(2,1)S(1)}, bf16[2,256,1280]{2,1,0:T(8,128)(2,1)}, u32[]{:S(2)}) %copy-start) | copy-done | bytes 1310744
  1.3 0.0 copy-start.1
  1.3 1.3 %copy-done.1 = f32[5,256,256]{2,1,0:T(8,128)S(1)} copy-done((f32[5,256,256]{2,1,0:T(8,128)S(1)}, f32[5,256,256]{2,1,0:T(8,128)}, u32[]{:S(2)}) %copy-start.1) | copy-done | bytes 1310744
  2.6 0.0 copy-start.2
  2.6 1.1 %copy-done.2 = bf16[256,1280]{1,0:T(8,128)(2,1)S(1)} copy-done((bf16[256,1280]{1,0:T(8,128)(2,1)S(1)}, bf16[256,1280]{1,0:T(8,128)(2,1)}, u32[]{:S(2)}) %copy-start.2) | copy-done | bytes 655384
  3.7 0.0 copy-start.3
  3.7 1.1 %copy-done.3 = bf16[256,1280]{1,0:T(8,128)(2,1)S(1)} copy-done((bf16[256,1280]{1,0:T(8,128)(2,1)S(1)}, bf16[256,1280]{1,0:T(8,128)(2,1)}, u32[]{:S(2)}) %copy-start.3) | copy-done | bytes 655384
  4.8 0.0 copy-start.4
  4.8 0.7 copy-done.4
  5.5 93.0 %shard_map.73 = bf16[2,64,5120]{2,1,0:T(8,128)(2,1)S(1)} custom-call(bf16[2,256,1280]{2,1,0:T(8,128)(2,1)S(1)} %copy-done, bf16[256,1280]{1,0:T(8,128)(2,1)S(1)} %copy-done.2, bf16[256,1280]{1,0:T(8,128)(2,1)S(1)} %copy-done.3, f32[5,256]{1,0:T(8,128)S(1)} %copy-done.4, f32[5,256,256]{2,1,0:T(8,128)S(1)} %copy-done.1, f32[5,256,256]{2,1,0:T(8,128)} %u_in.1, ...), custom_call_target="tpu_custom_call" | custom-call | tf_op jit(solution)/shard_map/pallas_call | solution.py:363
  98.5 1.1 %copy.9 = bf16[2,64,5120]{2,1,0:T(8,128)(2,1)} copy(bf16[2,64,5120]{2,1,0:T(8,128)(2,1)S(1)} %shard_map.73) | data formatting | bytes 2621440
Async XLA Ops:
  0.0 1.3 %copy-start = (bf16[2,256,1280]{2,1,0:T(8,128)(2,1)S(1)}, bf16[2,256,1280]{2,1,0:T(8,128)(2,1)}, u32[]{:S(2)}) copy-start(bf16[2,256,1280]{2,1,0:T(8,128)(2,1)} %q_in.1) | copy-start | bytes 3932164
  1.3 1.3 %copy-start.1 = (f32[5,256,256]{2,1,0:T(8,128)S(1)}, f32[5,256,256]{2,1,0:T(8,128)}, u32[]{:S(2)}) copy-start(f32[5,256,256]{2,1,0:T(8,128)} %g_in.1) | copy-start | bytes 3932164
  2.6 1.1 %copy-start.2 = (bf16[256,1280]{1,0:T(8,128)(2,1)S(1)}, bf16[256,1280]{1,0:T(8,128)(2,1)}, u32[]{:S(2)}) copy-start(bf16[256,1280]{1,0:T(8,128)(2,1)} %k_in.1) | copy-start | bytes 1966084
  3.7 1.1 %copy-start.3 = (bf16[256,1280]{1,0:T(8,128)(2,1)S(1)}, bf16[256,1280]{1,0:T(8,128)(2,1)}, u32[]{:S(2)}) copy-start(bf16[256,1280]{1,0:T(8,128)(2,1)} %v_in.1) | copy-start | bytes 1966084
  4.8 0.7 copy-start.4

commit v2 on v1

--- a/solution.py
+++ b/solution.py
@@ -10,7 +10,8 @@
 NS_STEPS = 3
 KINDS = 3
 PIECES = 2
-LAG = 2
+EXTRA = 2
+DEPTH = 4
 
 coef_first = 3.4445
 coef_second = -4.775
@@ -139,6 +140,20 @@
             wn.at[m, part], wn.at[m, part], ap_s.at[j, g], ap_r.at[j, g],
             device_id=partner, device_id_type=MESH,
         )
+
+    def launch(make, j, g):
+        before = j + 2 * ((g - DEPTH) // PIECES)
+
+        @pl.when(before >= 0)
+        def _():
+            make(before, (g - DEPTH) % PIECES).wait_send()
+
+        make(j, g).start()
+
+    def land(make, j, g):
+        @pl.when(mine(j + 2 * ((g + DEPTH) // PIECES)) >= count)
+        def _():
+            make(j, g).wait_send()
 
     def wide(h):
         return pl.ds(pl.multiple_of((hd * heads + h) * size, size), size)
@@ -228,7 +243,7 @@
         def _():
             cs[j] = (gb[mine(j)].astype(F32) + pb[j].astype(F32)).astype(BF)
             for g in range(PIECES):
-                chain(j, g).start()
+                launch(chain, j, g)
 
     def pass_step(j):
         @pl.when(jnp.logical_not(is_start(j)) & jnp.logical_not(is_owner(j)))
@@ -241,15 +256,24 @@
                     + pb[j, part].astype(F32)
                     + cr[j, part].astype(F32)
                 ).astype(BF)
-                chain(j, g).start()
-
-    @pl.loop(0, 2 * heads)
+                launch(chain, j, g)
+
+    lag = EXTRA + max(
+        min((2 * j + 1) // KINDS, heads - 1) + 1 - (j // 2 + 1) for j in range(pairs)
+    )
+    turns = (pairs - 1) // 2 + nz - 1
+    total = max(2 * heads, turns + lag)
+
+    def reach(j):
+        return jnp.where(side(j) == 0, nz - 1 - z, z)
+
+    @pl.loop(0, total)
     def _(t):
         @pl.when(t < heads)
         def _():
             gradients(t)
 
-        @pl.when(t >= heads)
+        @pl.when((t >= heads) & (t < 2 * heads))
         def _():
             first(t - heads)
 
@@ -257,9 +281,13 @@
         def _():
             own(t - 1, start_step)
 
-        @pl.when((t >= LAG) & (t < heads + LAG))
-        def _():
-            own(t - LAG, pass_step)
+        for s in range(2):
+            i = t - lag - reach(s)
+            j = 2 * i + s
+
+            @pl.when((i >= 0) & (j < pairs) & (mine(j) < count))
+            def _():
+                pass_step(j)
 
     @pl.loop(0, pairs)
     def _(j):
@@ -280,7 +308,7 @@
                 x = coef_first * x + mm(xb, poly.astype(BF))
             wn[m] = (wf[lax.rem(m, KINDS), m // KINDS] - x).astype(BF)
             for g in range(PIECES):
-                spread(j, g).start()
+                launch(spread, j, g)
                 across(j, g, m).start()
 
     def second(h):
@@ -292,54 +320,65 @@
                 for g in range(PIECES):
                     across(m // 2, g, m).wait_recv()
 
-        @pl.when(h >= 0)
-        def _():
-            wait_load(h, (6,))
-            base = KINDS * h
-            ob[1, h] = fast_apply(qb[1, h], wn[base], wn[base + 1], wn[base + 2])
-            deal_all(1, h)
+        wait_load(h, (6,))
+        base = KINDS * h
+        ob[1, h] = fast_apply(qb[1, h], wn[base], wn[base + 1], wn[base + 2])
+        deal_all(1, h)
+
+    def relay(j):
+        m = mine(j)
+        for g in range(PIECES):
+            spread(j, g).wait_recv()
+
+            @pl.when(jnp.logical_not(is_start(j)))
+            def _():
+                launch(spread, j, g)
+
+            across(j, g, m).start()
+
+    def away(j):
+        return jnp.where(side(j) == 0, z, nz - 1 - z)
+
+    @pl.loop(0, (pairs - 1) // 2 + nz)
+    def _(t):
+        for s in range(2):
+            i = t - away(s)
+            j = 2 * i + s
+
+            @pl.when((i >= 0) & (j < pairs) & (mine(j) < count) & jnp.logical_not(is_owner(j)))
+            def _():
+                relay(j)
+
+        @pl.loop(0, heads)
+        def _(h):
+            top = (KINDS * h + KINDS - 1) // 2
+            below = top - 1
+            due = jnp.maximum(top // 2 + away(top), below // 2 + away(below))
+
+            @pl.when(due == t)
+            def _():
+                second(h)
 
     @pl.loop(0, pairs)
     def _(j):
         m = mine(j)
 
-        @pl.when((m < count) & jnp.logical_not(is_owner(j)))
+        @pl.when(2 * j + 1 - lane < count)
+        def _():
+            swap(j).wait_send()
+
+        @pl.when(m < count)
         def _():
             for g in range(PIECES):
-                spread(j, g).wait_recv()
+                across(j, g, m).wait_send()
+
+                @pl.when(jnp.logical_not(is_owner(j)))
+                def _():
+                    land(chain, j, g)
 
                 @pl.when(jnp.logical_not(is_start(j)))
                 def _():
-                    spread(j, g).start()
-
-                across(j, g, m).start()
-
-        h = jnp.maximum(2 * j - 1, 0) // KINDS
-
-        @pl.when((j >= 1) & (h < heads) & ((KINDS * h + KINDS - 1) // 2 == j))
-        def _():
-            second(h)
-
-    @pl.loop(0, pairs)
-    def _(j):
-        m = mine(j)
-
-        @pl.when(2 * j + 1 - lane < count)
-        def _():
-            swap(j).wait_send()
-
-        @pl.when(m < count)
-        def _():
-            for g in range(PIECES):
-                across(j, g, m).wait_send()
-
-                @pl.when(jnp.logical_not(is_owner(j)))
-                def _():
-                    chain(j, g).wait_send()
-
-                @pl.when(jnp.logical_not(is_start(j)))
-                def _():
-                    spread(j, g).wait_send()
+                    land(spread, j, g)
 
     for b in range(2):
         @pl.loop(0, heads)
@@ -390,7 +429,7 @@
                 dma((2, heads)),
             ],
             compiler_params=pltpu.CompilerParams(
-                collective_id=0, has_side_effects=True, vmem_limit_bytes=48 << 20
+                collective_id=0, has_side_effects=True, vmem_limit_bytes=67043328
             ),
         )(queries, key_rows, value_rows, step_rates, gate_fast, up_fast, down_fast)
 

time: 99.9 us -> 53.2 us (0.53)
  Pallas kernels: 93 us -> 50.6 us
  local copies, waits for them, and re-layouts: 6.56 us -> 2.46 us
    pallas_call x1, Pallas kernels: 93 us -> 50.6 us  [local(): pl.pallas_call(functools.partial(kernel, nh, nz), out_shape=jax.ShapeDtyp...]
    unnamed x11 -> x1, local copies, waits for them, and re-layouts: 6.56 us -> 2.46 us
where the time goes in v2:
time: 53.2 us; the launch traced here: 53 us
  Pallas kernels  50.6 us (95%)
  local copies, waits for them, and re-layouts  2.46 us (5%)
    pallas_call x1, Pallas kernels, local(): pl.pallas_call(functools.partial(kernel, nh, nz), out_shape=jax.ShapeDtyp...  50.6 us
    unnamed x1, local copies, waits for them, and re-layouts  2.46 us

profile of v2, /device:TPU:0, one launch (start us, length us, event | category | flops | bytes accessed | tf_op | source)
XLA Modules:
  0.0 53.0 jit_solution(1849870849797316291)
XLA Ops:
  0.0 50.6 %shard_map.73 = bf16[2,64,5120]{2,1,0:T(8,128)(2,1)} custom-call(bf16[2,256,1280]{2,1,0:T(8,128)(2,1)} %q_in.1, bf16[256,1280]{1,0:T(8,128)(2,1)} %k_in.1, bf16[256,1280]{1,0:T(8,128)(2,1)} %v_in.1, f32[5,256]{1,0:T(8,128)} %rates.1, f32[5,256,256]{2,1,0:T(8,128)} %g_in.1, f32[5,256,256]{2,1,0:T(8,128)} %u_in.1, f32[5,256,256]{2,1,0:T(8,128)} %d_in.1), custom_call_target="tpu_custom_call" | custom-call | tf_op jit(solution)/shard_map/pallas_call | solution.py:402
  50.6 2.5 %copy.9 = bf16[2,64,5120]{2,1,0:T(8,128)(2,1)} copy(bf16[2,64,5120]{2,1,0:T(8,128)(2,1)} %shard_map.73) | data formatting | bytes 2621440

commit v3 on v2

--- a/solution.py
+++ b/solution.py
@@ -9,9 +9,9 @@
 
 NS_STEPS = 3
 KINDS = 3
-PIECES = 2
-EXTRA = 2
-DEPTH = 4
+PIECES = 4
+EXTRA = 3
+DEPTH = 16
 
 coef_first = 3.4445
 coef_second = -4.775

time: 53.2 us -> 53.9 us (1.013)
  Pallas kernels: 50.6 us -> 51.2 us
    pallas_call x1, Pallas kernels: 50.6 us -> 51.2 us  [local(): pl.pallas_call(functools.partial(kernel, nh, nz), out_shape=jax.ShapeDtyp...]
where the time goes in v3:
time: 53.9 us; the launch traced here: 53.7 us
  Pallas kernels  51.2 us (95%)
  local copies, waits for them, and re-layouts  2.46 us (5%)
    pallas_call x1, Pallas kernels, local(): pl.pallas_call(functools.partial(kernel, nh, nz), out_shape=jax.ShapeDtyp...  51.2 us
    unnamed x1, local copies, waits for them, and re-layouts  2.46 us

profile of v3, /device:TPU:0, one launch (start us, length us, event | category | flops | bytes accessed | tf_op | source)
XLA Modules:
  0.0 53.7 jit_solution(14760027739187180986)
XLA Ops:
  0.0 51.2 %shard_map.73 = bf16[2,64,5120]{2,1,0:T(8,128)(2,1)} custom-call(bf16[2,256,1280]{2,1,0:T(8,128)(2,1)} %q_in.1, bf16[256,1280]{1,0:T(8,128)(2,1)} %k_in.1, bf16[256,1280]{1,0:T(8,128)(2,1)} %v_in.1, f32[5,256]{1,0:T(8,128)} %rates.1, f32[5,256,256]{2,1,0:T(8,128)} %g_in.1, f32[5,256,256]{2,1,0:T(8,128)} %u_in.1, f32[5,256,256]{2,1,0:T(8,128)} %d_in.1), custom_call_target="tpu_custom_call" | custom-call | tf_op jit(solution)/shard_map/pallas_call | solution.py:402
  51.3 2.5 %copy.9 = bf16[2,64,5120]{2,1,0:T(8,128)(2,1)} copy(bf16[2,64,5120]{2,1,0:T(8,128)(2,1)} %shard_map.73) | data formatting | bytes 2621440
